TPU v7x, 32 devices: a whole 2x2x4 slice. The times are simulated.
32 devices in a mesh: dp: 16 (over z, y, core), mp: 2 (over x).
Axes of the slice: x: 2, y: 2, z: 4, core: 2. Of those that a mesh axis runs over, the one named last changes fastest.
Arguments:
- tokens: bfloat16 [2048, 2048], P('dp', 'mp'), may hold values from -32 to 32
- lengths: int32 [4], replicated, may hold values from 1 to 1536, 2048 in all
- keep_mask: int32 [2048], replicated, may hold values 0 or 1
- routes: int32 [2048, 8], P('dp'), may hold values from 0 to 63, all different within a row; in each aligned block of 128 rows (0 to 127, 128 to 255, ...) at most 32 rows name the same one
- attention_gain: float32 [2048], replicated, may hold values from 0.1 to 1.9
- mixture_gain: float32 [2048], P('mp'), may hold values from 0.1 to 1.9
- query_gain: float32 [128], replicated, may hold values from 0.5 to 8, as said below
- key_gain: float32 [128], replicated, may hold values from 0.5 to 8, as said below
- query_weight: bfloat16 [2048, 2048], P('dp', 'mp'), may hold values from -0.125 to 0.125
- key_weight: bfloat16 [2048, 2048], P('dp', 'mp'), may hold values from -0.125 to 0.125
- value_weight: bfloat16 [2048, 2048], P('dp', 'mp'), may hold values from -0.125 to 0.125
- output_weight: bfloat16 [2048, 2048], P('mp', 'dp'), may hold values from -0.1875 to 0.1875
- router_weight: float32 [2048, 64], P('mp'), may hold values from -0.125 to 0.125
- expert_gate: bfloat16 [16, 2048, 4096], P('dp', None, 'mp'), may hold values from -0.125 to 0.125
- expert_up: bfloat16 [16, 2048, 4096], P('dp', None, 'mp'), may hold values from -0.125 to 0.125
- expert_down: bfloat16 [16, 4096, 2048], P('dp', 'mp'), may hold values from -0.25 to 0.25
Outputs:
- layer_output: bfloat16 [2048, 2048], P('dp', 'mp')
Inputs may be any that keep to these rules, and one draw needn't show every extreme that they name: The lengths sum to 2048; exactly one is 1536. `routes`: each row names 8 different experts. Within each aligned block of 128 rows (the rows of one index of dp) no expert is named by more than 32 rows, a bound that some block reaches. `query_gain`: Positive. `key_gain`: Positive.
All inputs are finite; a program needn't handle non-finite values.
Results may differ from a plain program's by a relative error of at most 0.012.
The roundings to bfloat16 on the way count: a program that leaves them out, or rounds other values in their place, can miss the bound.
Values may be sent and summed in bfloat16 or wider, within the bound.
A program may use at most 128 MiB of HBM per device.

v0:
```python
import jax
import jax.numpy as jnp
from jax import lax
from jax.sharding import PartitionSpec as P

D = 2048
HEAD_DIM = 128
FF = 1024
EXPERTS = 64
TOPK = 8
CAP = 32
EPS = 1e-06
ROPE_BASE = 10000.0
NEG = -1e30


def rope_tables(position):
    halves = HEAD_DIM // 2
    exponent = jnp.arange(halves, dtype=jnp.float32) * (2.0 / HEAD_DIM)
    frequency = jnp.power(jnp.float32(ROPE_BASE), -exponent)
    angle = position.astype(jnp.float32)[:, None] * frequency[None, :]
    cos_table = jnp.cos(angle)
    sin_table = jnp.sin(angle)
    return (jnp.concatenate([cos_table, cos_table], 1), jnp.concatenate([sin_table, sin_table], 1))


def head_prep(projected, head_gain, cos_table, sin_table):
    row_count = projected.shape[0]
    per_head = projected.reshape(row_count, -1, HEAD_DIM)
    normed = (
        per_head * lax.rsqrt(jnp.mean(per_head * per_head, axis=2, keepdims=True) + EPS) * head_gain
    )
    halves = HEAD_DIM // 2
    rotated = jnp.concatenate([-normed[:, :, halves:], normed[:, :, :halves]], 2)
    turned = normed * cos_table[:, None, :] + rotated * sin_table[:, None, :]
    return turned.reshape(row_count, -1).astype(jnp.bfloat16)


def segment_info(lengths, first_row, row_count):
    request_end = jnp.cumsum(lengths)
    request_start = request_end - lengths
    global_row = first_row + jnp.arange(row_count, dtype=jnp.int32)
    segment = jnp.sum((request_end[None, :] <= global_row[:, None]).astype(jnp.int32), axis=1)
    chosen = segment[:, None] == jnp.arange(lengths.shape[0], dtype=jnp.int32)[None, :]
    begin = jnp.sum(jnp.where(chosen, request_start[None, :], 0), axis=1)
    return (segment, global_row - begin, global_row)


def local(
    tokens,
    lengths,
    keep_mask,
    routes,
    attention_gain,
    mixture_gain,
    query_gain,
    key_gain,
    query_weight,
    key_weight,
    value_weight,
    output_weight,
    router_weight,
    expert_gate,
    expert_up,
    expert_down,
):
    tok_rows = tokens.shape[0]
    dp_count = lax.axis_size("dp")
    first_row = lax.axis_index("dp") * tok_rows
    full_tokens = lax.all_gather(tokens, "mp", axis=1, tiled=True)
    xfloat = full_tokens.astype(jnp.float32)
    normed_in = (
        xfloat * lax.rsqrt(jnp.mean(xfloat * xfloat, axis=1, keepdims=True) + EPS) * attention_gain
    ).astype(jnp.bfloat16)
    segment, position, global_row = segment_info(lengths, first_row, tok_rows)
    cos_table, sin_table = rope_tables(position)
    local_width = query_weight.shape[1]
    query_proj = jnp.dot(
        normed_in,
        lax.all_gather(query_weight, "dp", axis=0, tiled=True),
        preferred_element_type=jnp.float32,
    )
    key_proj = jnp.dot(
        normed_in,
        lax.all_gather(key_weight, "dp", axis=0, tiled=True),
        preferred_element_type=jnp.float32,
    )
    value_proj = jnp.dot(
        normed_in,
        lax.all_gather(value_weight, "dp", axis=0, tiled=True),
        preferred_element_type=jnp.float32,
    )
    queries = head_prep(query_proj, query_gain, cos_table, sin_table)
    key_heads = head_prep(key_proj, key_gain, cos_table, sin_table)
    value_heads = value_proj.astype(jnp.bfloat16)
    local_heads = local_width // HEAD_DIM
    query_split = queries.reshape(tok_rows, local_heads, HEAD_DIM)
    seg_low = segment[0]
    seg_high = segment[tok_rows - 1]
    scale = HEAD_DIM ** (-0.5)
    start_state = (
        jnp.full((local_heads, tok_rows), NEG, jnp.float32),
        jnp.zeros((local_heads, tok_rows), jnp.float32),
        jnp.zeros((tok_rows, local_heads, HEAD_DIM), jnp.float32),
    )
    key_piece = lax.all_gather(key_heads, "dp", axis=0, tiled=True)
    value_piece = lax.all_gather(value_heads, "dp", axis=0, tiled=True)
    piece_rows = key_piece.shape[0]
    key_seg, unused_pos, key_row = segment_info(lengths, jnp.int32(0), piece_rows)

    def compute(state_now):
        run_max, run_sum, run_acc = state_now
        key_split = key_piece.reshape(piece_rows, local_heads, HEAD_DIM)
        value_split = value_piece.reshape(piece_rows, local_heads, HEAD_DIM)
        scores = (
            jnp.einsum("thd,shd->hts", query_split, key_split, preferred_element_type=jnp.float32)
            * scale
        )
        visible = (segment[:, None] == key_seg[None, :]) & (
            (keep_mask[None, :] == 1) | (global_row[:, None] == key_row[None, :])
        )
        masked = jnp.where(visible[None], scores, NEG)
        new_max = jnp.maximum(run_max, jnp.max(masked, axis=2))
        factor = jnp.exp(run_max - new_max)
        weights = jnp.where(visible[None], jnp.exp(masked - new_max[:, :, None]), 0.0)
        new_sum = jnp.sum(weights, axis=2)
        mixed = jnp.einsum(
            "hts,shd->thd",
            weights.astype(jnp.bfloat16),
            value_split,
            preferred_element_type=jnp.float32,
        )
        new_acc = run_acc * factor.T[:, :, None] + mixed
        return (new_max, new_sum, new_acc)

    touches = (key_seg[piece_rows - 1] >= seg_low) & (key_seg[0] <= seg_high)
    final_max, final_sum, final_acc = lax.cond(
        touches, compute, lambda state_now: state_now, start_state
    )
    attended = (
        (final_acc / final_sum.T[:, :, None]).reshape(tok_rows, local_width).astype(jnp.bfloat16)
    )
    partial_out = jnp.dot(
        attended,
        lax.all_gather(output_weight, "dp", axis=1, tiled=True),
        preferred_element_type=jnp.float32,
    )
    summed_out = lax.psum_scatter(partial_out, "mp", scatter_dimension=1, tiled=True)
    residual = (tokens.astype(jnp.float32) + summed_out).astype(jnp.bfloat16)
    hfloat = residual.astype(jnp.float32)
    scaled = hfloat * mixture_gain
    partial_logits = jnp.dot(scaled, router_weight, precision=lax.Precision.HIGHEST)
    square_sum, logit_sum = lax.psum((jnp.sum(hfloat * hfloat, axis=1), partial_logits), "mp")
    inverse = lax.rsqrt(square_sum / D + EPS)[:, None]
    mixed_in = (scaled * inverse).astype(jnp.bfloat16)
    logits = logit_sum * inverse
    picked = jnp.take_along_axis(logits, routes, axis=1)
    sigmoid_vals = jax.nn.sigmoid(picked)
    route_weight = sigmoid_vals / jnp.sum(sigmoid_vals, axis=1, keepdims=True)
    onehot = jnp.sum(
        (routes[:, :, None] == jnp.arange(EXPERTS, dtype=jnp.int32)[None, None, :]).astype(
            jnp.int32
        ),
        axis=1,
    )
    before = jnp.cumsum(onehot, axis=0) - onehot
    slot = jnp.take_along_axis(before, routes, axis=1)
    target = routes * CAP + slot
    token_ids = jnp.repeat(jnp.arange(tok_rows, dtype=jnp.int32), TOPK)
    source = jnp.full((EXPERTS * CAP,), tok_rows, jnp.int32).at[target.reshape(-1)].set(token_ids)
    exp_local = EXPERTS // dp_count
    gate_local = expert_gate[0]
    up_local = expert_up[0]
    down_local = expert_down[0]
    unit_count = gate_local.shape[1]
    mp_index = lax.axis_index("mp")
    full_in = lax.all_gather(mixed_in, "mp", axis=1, tiled=True)
    padded = jnp.concatenate([full_in, jnp.zeros((1, full_in.shape[1]), jnp.bfloat16)], 0)
    sending = padded[source].reshape(dp_count, exp_local, CAP, full_in.shape[1])
    rows_in = lax.all_to_all(sending, "dp", split_axis=0, concat_axis=0, tiled=True)
    if unit_count <= FF:
        owners = FF // unit_count
        expert_index = mp_index // owners
        own_rows = lax.dynamic_index_in_dim(rows_in, expert_index, 1, keepdims=False)
        gate_val = jnp.einsum(
            "scd,dh->sch", own_rows, gate_local, preferred_element_type=jnp.float32
        )
        up_val = jnp.einsum("scd,dh->sch", own_rows, up_local, preferred_element_type=jnp.float32)
        hidden = (jax.nn.silu(gate_val) * up_val).astype(jnp.bfloat16)
        own_part = jnp.einsum("sch,hd->scd", hidden, down_local, preferred_element_type=jnp.float32)
        selector = (jnp.arange(exp_local, dtype=jnp.int32) == expert_index).astype(jnp.float32)
        partial_rows = own_part[:, None, :, :] * selector[None, :, None, None]
    else:
        held = unit_count // FF
        first_expert = mp_index * held
        own_rows = lax.dynamic_slice_in_dim(rows_in, first_expert, held, 1)
        gate_val = jnp.einsum(
            "secd,def->secf",
            own_rows,
            gate_local.reshape(gate_local.shape[0], held, FF),
            preferred_element_type=jnp.float32,
        )
        up_val = jnp.einsum(
            "secd,def->secf",
            own_rows,
            up_local.reshape(up_local.shape[0], held, FF),
            preferred_element_type=jnp.float32,
        )
        hidden = (jax.nn.silu(gate_val) * up_val).astype(jnp.bfloat16)
        own_part = jnp.einsum(
            "secf,efd->secd",
            hidden,
            down_local.reshape(held, FF, down_local.shape[1]),
            preferred_element_type=jnp.float32,
        )
        empty_rows = jnp.zeros(
            (rows_in.shape[0], exp_local, rows_in.shape[2], own_part.shape[3]), jnp.float32
        )
        partial_rows = lax.dynamic_update_slice_in_dim(empty_rows, own_part, first_expert, 1)
    summed_rows = lax.psum_scatter(
        partial_rows.astype(jnp.bfloat16), "mp", scatter_dimension=3, tiled=True
    )
    returned = lax.all_to_all(summed_rows, "dp", split_axis=0, concat_axis=0, tiled=True)
    flat = returned.reshape(EXPERTS * CAP, local_width)
    gathered = flat[target]
    mixture = jnp.sum(gathered.astype(jnp.float32) * route_weight[:, :, None], axis=1)
    return (hfloat + mixture).astype(jnp.bfloat16)


def solution(mesh):
    return jax.shard_map(
        local,
        mesh=mesh,
        in_specs=(
            P("dp", "mp"),
            P(),
            P(),
            P("dp", None),
            P(),
            P("mp"),
            P(),
            P(),
            P("dp", "mp"),
            P("dp", "mp"),
            P("dp", "mp"),
            P("mp", "dp"),
            P("mp", None),
            P("dp", None, "mp"),
            P("dp", None, "mp"),
            P("dp", "mp", None),
        ),
        out_specs=P("dp", "mp"),
        check_vma=False,
    )
```

profile of v0, /device:TPU:13, one launch (start us, length us, event | category | flops | bytes accessed | tf_op | source)
XLA Modules:
  0.0 811.3 jit_solution(14257861319533035457)
XLA Ops:
  6.5 0.7 all-gather.9.cloned.1.call-update
  7.3 0.7 all-gather.7.cloned.1.call-update
  8.1 0.7 all-gather.13.cloned.1.call-update
  8.8 0.8 reduce-window.8
  9.7 0.7 bitcast_subtract_fusion
  10.5 0.3 multiply_cosine_fusion
  10.9 8.1 all_gather.24
  19.0 0.2 fusion.44
  19.2 0.7 broadcast_bitcast_fusion
  19.9 41.0 %all-gather.9.cloned.1.call-done = bf16[2048,1024]{1,0:T(8,128)(2,1)} async-done(((bf16[128,1024]{1,0:T(8,128)(2,1)}), bf16[2048,1024]{1,0:T(8,128)(2,1)}) %all-gather.9.cloned.1.call-update) | async-done | bytes 4194320 | tf_op jit(solution)/shard_map/all_gather | solution.py:85
  60.9 3.0 fusion.67
  64.0 0.2 multiply_reduce_fusion
  64.3 0.1 copy.97
  64.4 47.8 %all-gather.7.cloned.1.call-done = bf16[2048,1024]{1,0:T(8,128)(2,1)} async-done(((bf16[128,1024]{1,0:T(8,128)(2,1)}), bf16[2048,1024]{1,0:T(8,128)(2,1)}) %all-gather.7.cloned.1.call-update) | async-done | bytes 4194320 | tf_op jit(solution)/shard_map/all_gather | solution.py:80
  112.1 2.9 fusion.69
  115.2 0.2 multiply_reduce_fusion.1
  115.5 0.1 copy.95
  115.6 0.2 multiply_multiply_fusion
  115.8 0.2 multiply_multiply_fusion.1
  116.0 0.4 slice_negate_fusion
  116.4 0.4 maximum_multiply_fusion.1
  116.8 0.2 mul.217
  117.0 0.2 mul.239
  117.2 1.2 fusion.56
  118.6 44.8 %all-gather.13.cloned.1.call-done = bf16[2048,1024]{1,0:T(8,128)(2,1)} async-done(((bf16[128,1024]{1,0:T(8,128)(2,1)}), bf16[2048,1024]{1,0:T(8,128)(2,1)}) %all-gather.13.cloned.1.call-update) | async-done | bytes 4194320 | tf_op jit(solution)/shard_map/all_gather | solution.py:90
  163.4 3.6 convolution_convert_fusion
  167.1 0.5 all-gather.17.cloned.1.call-update
  167.8 0.7 fusion.71
  171.0 43.5 %all-gather.11.cloned.1.call-done = bf16[2048,1024]{1,0:T(8,128)(2,1)} async-done(((bf16[128,1024]{1,0:T(8,128)(2,1)}), bf16[2048,1024]{1,0:T(8,128)(2,1)}) %all-gather.11.cloned.1.call-update) | async-done | bytes 4194320 | tf_op jit(solution)/shard_map/all_gather | solution.py:106
  214.5 51.1 %all-gather.15.cloned.1.call-done = bf16[2048,1024]{1,0:T(8,128)(2,1)} async-done(((bf16[128,1024]{1,0:T(8,128)(2,1)}), bf16[2048,1024]{1,0:T(8,128)(2,1)}) %all-gather.15.cloned.1.call-update) | async-done | bytes 4194320 | tf_op jit(solution)/shard_map/all_gather | solution.py:107
  265.6 16.5 %conditional.1 = (f32[8,128]{1,0:T(8,128)S(1)}, f32[128,8,128]{0,2,1:T(8,128)S(1)}) conditional(s32[]{:T(128)} %bitcast.4, () %tuple.13, (s32[128]{0:T(128)S(1)}, s32[2048]{0:T(1024)S(1)}, s32[2048]{0:T(1024)S(1)}, s32[]{:T(128)}, s32[128]{0:T(128)S(1)}, /*index=5*/s32[2048]{0:T(1024)S(1)}, bf16[128,1024]{1,0:T(8,128)(2,1)S(1)}, ...), branch_computations={%region_7.8_spmd, %region_8.11_spmd} | conditional | flops 1102187648 | bytes 86833224 | solution.py:137
  265.6 0.4 or_and_fusion
  266.0 4.6 fusion
  270.6 3.2 copy-done.2
  273.8 3.3 fusion.19
  277.1 0.2 copy.119
  277.3 4.7 fusion.2
  282.1 35.4 %all-gather.17.cloned.1.call-done = bf16[1024,2048]{1,0:T(8,128)(2,1)} async-done(((bf16[1024,128]{1,0:T(8,128)(2,1)}), bf16[1024,2048]{1,0:T(8,128)(2,1)}) %all-gather.17.cloned.1.call-update) | async-done | bytes 4194320 | tf_op jit(solution)/shard_map/all_gather | solution.py:145
  317.5 3.9 fusion.73
  321.8 0.2 reduce_window_sum.19
  322.0 7.1 gather_fusion.2
  329.3 0.1 copy.103
  329.6 4.3 scatter_custom_fusion
  334.0 8.4 %reduce-scatter.3.cloned.1.call-done = f32[128,1024]{1,0:T(8,128)} async-done(((f32[128,2048]{1,0:T(8,128)}), f32[128,1024]{1,0:T(8,128)}) %reduce-scatter.3.cloned.1.call-update) | async-done | bytes 524304 | tf_op jit(solution)/shard_map/reduce_scatter | solution.py:148
  342.4 1.2 fusion.54
  343.6 0.7 fusion.47
  344.3 5.5 all-reduce.1
  349.9 5.9 all_gather.31
  355.9 11.0 %gather_fusion = bf16[2048,2048]{1,0:T(8,128)(2,1)} fusion(bf16[129,2048]{1,0:T(8,128)(2,1)S(1)} %concatenate.19, s32[2048]{0:T(1024)S(1)} %fusion.62), kind=kCustom, calls=%fused_computation | custom fusion | bytes 16785408 | tf_op jit(solution)/shard_map/gather | solution.py:179
  366.9 9.5 %all-to-all-start = ((bf16[16,4,32,2048]{3,2,1,0:T(8,128)(2,1)}), bf16[16,4,32,2048]{3,2,1,0:T(8,128)(2,1)}, u32[]{:S(2)}, u32[]{:S(2)}) async-start(bf16[16,4,32,2048]{3,2,1,0:T(8,128)(2,1)} %bitcast.130), calls=%async_computation.1 | async-start | bytes 16777216 | tf_op jit(solution)/shard_map/all_to_all | solution.py:180
  376.5 14.4 %reshape_squeeze.10 = bf16[2048,2,1024]{2,1,0:T(2,128)(2,1)} reshape(bf16[1,2048,2048]{2,1,0:T(8,128)(2,1)} %param.32) | data formatting | bytes 16777216 | tf_op jit(solution)/shard_map/reshape;squeeze | solution.py:206
  390.9 14.5 %reshape_squeeze.9 = bf16[2048,2,1024]{2,1,0:T(2,128)(2,1)} reshape(bf16[1,2048,2048]{2,1,0:T(8,128)(2,1)} %param.31) | data formatting | bytes 16777216 | tf_op jit(solution)/shard_map/reshape;squeeze | solution.py:200
  405.4 153.3 %all-to-all-done = bf16[16,4,32,2048]{3,2,1,0:T(8,128)(2,1)} async-done(((bf16[16,4,32,2048]{3,2,1,0:T(8,128)(2,1)}), bf16[16,4,32,2048]{3,2,1,0:T(8,128)(2,1)}, u32[]{:S(2)}, u32[]{:S(2)}) %all-to-all-start) | async-done | bytes 8388640 | tf_op jit(solution)/shard_map/all_to_all | solution.py:180
  558.8 11.3 %fusion.29 = f32[2,16,32,1024]{3,2,1,0:T(8,128)} fusion(bf16[2048,2,1024,1]{2,1,0,3:T(2,128)(2,1)} %bitcast.132, bf16[16,4,32,2048]{3,2,1,0:T(8,128)(2,1)} %all-to-all-done, s32[]{:T(128)S(6)} %select_n.52), kind=kOutput, calls=%fused_computation.32 | convolution fusion | flops 4294967296 | bytes 16777220 | tf_op jit(solution)/shard_map/secd,def->secf/dot_general | solution.py:203
  570.0 20.3 %convolution_bitcast_fusion = bf16[16,2,32,2048]{3,2,0,1:T(8,128)(2,1)} fusion(bf16[2,1024,2048,1]{2,1,3,0:T(8,128)(2,1)} %bitcast.147, f32[2,16,32,1024]{3,2,1,0:T(8,128)} %fusion.29, bf16[2048,2,1024,1]{2,1,0,3:T(2,128)(2,1)} %bitcast.131, bf16[16,4,32,2048]{3,2,1,0:T(8,128)(2,1)} %all-to-all-done, s32[]{:T(128)S(6)} %select_n.52), kind=kOutput, calls=%fused_computation.37 | convolution fusion | flops 8596226048 | bytes 29360132 | tf_op jit(solution)/shard_map/secf,efd->secd/dot_general | solution.py:210
  590.3 4.3 broadcast_in_dim.70
  594.6 2.3 copy_dynamic-update-slice_fusion
  596.9 98.9 %reduce-scatter.5.cloned.1.call-done = bf16[16,4,32,1024]{3,2,1,0:T(8,128)(2,1)} async-done(((bf16[16,4,32,2048]{3,2,1,0:T(8,128)(2,1)}), bf16[16,4,32,1024]{3,2,1,0:T(8,128)(2,1)}) %reduce-scatter.5.cloned.1.call-update) | async-done | bytes 4194320 | tf_op jit(solution)/shard_map/reduce_scatter | solution.py:220
  695.8 6.3 all-to-all-start.1
  702.4 7.0 gather_fusion.3
  709.7 84.9 %all-to-all-done.1 = bf16[16,4,32,1024]{3,2,1,0:T(8,128)(2,1)} async-done(((bf16[16,4,32,1024]{3,2,1,0:T(8,128)(2,1)}), bf16[16,4,32,1024]{3,2,1,0:T(8,128)(2,1)}, u32[]{:S(2)}, u32[]{:S(2)}) %all-to-all-start.1) | async-done | bytes 4194336 | tf_op jit(solution)/shard_map/all_to_all | solution.py:223
  794.6 7.7 gather_fusion.1
  802.4 1.3 fusion.33
  803.7 0.8 fusion.55
  (82 shorter events, 2.6 us)
Async XLA Ops:
  6.5 337.1 %copy-start = (f32[1024,64]{0,1:T(8,128)S(1)}, f32[1024,64]{0,1:T(8,128)}, u32[]{:S(2)}) copy-start(f32[1024,64]{0,1:T(8,128)} %param.30) | copy-start | bytes 786436
  6.5 54.4 %all-gather.9.cloned.1.call-start = ((), (), s32[]{:S(2)}) async-start(), calls=%async_computation.5 | async-start | bytes 4456448 | tf_op jit(solution)/shard_map/all_gather | solution.py:85
  7.3 104.9 %all-gather.7.cloned.1.call-start = ((), (), s32[]{:S(2)}) async-start(), calls=%async_computation.4 | async-start | bytes 4456448 | tf_op jit(solution)/shard_map/all_gather | solution.py:80
  8.0 155.4 %all-gather.13.cloned.1.call-start = ((), (), s32[]{:S(2)}) async-start(), calls=%async_computation.7 | async-start | bytes 4456448 | tf_op jit(solution)/shard_map/all_gather | solution.py:90
  8.7 205.8 %all-gather.11.cloned.1.call-start = ((), (), s32[]{:S(2)}) async-start(), calls=%async_computation.6 | async-start | bytes 4456448 | tf_op jit(solution)/shard_map/all_gather | solution.py:106
  10.9 101.2 %copy-start.6 = (f32[2048]{0:T(1024)S(1)}, f32[2048]{0:T(1024)}, u32[]{:S(2)}) copy-start(f32[2048]{0:T(1024)} %param.22) | copy-start | bytes 24580
  63.9 51.7 %copy-start.9 = (f32[128]{0:T(128)S(1)}, f32[128]{0:T(128)}, u32[]{:S(2)}) copy-start(f32[128]{0:T(128)} %param.25) | copy-start | bytes 1540
  64.2 51.6 %copy-start.10 = (f32[128]{0:T(128)S(1)}, f32[128]{0:T(128)}, u32[]{:S(2)}) copy-start(f32[128]{0:T(128)} %param.24) | copy-start | bytes 1540
  117.2 148.4 %copy-start.8 = (s32[2048]{0:T(1024)S(1)}, s32[2048]{0:T(1024)}, u32[]{:S(2)}) copy-start(s32[2048]{0:T(1024)} %param.20) | copy-start | bytes 24580
  118.5 147.1 %all-gather.15.cloned.1.call-start = ((), (), s32[]{:S(2)}) async-start(), calls=%async_computation.8 | async-start | bytes 4456448 | tf_op jit(solution)/shard_map/all_gather | solution.py:107
  167.1 150.5 %all-gather.17.cloned.1.call-start = ((), (), s32[]{:S(2)}) async-start(), calls=%async_computation.9 | async-start | bytes 4456448 | tf_op jit(solution)/shard_map/all_gather | solution.py:145
  167.7 174.8 %reduce-scatter.3.cloned.1.call-start = ((), (), s32[]{:S(2)}) async-start(), calls=%async_computation.10 | async-start | bytes 1572864 | tf_op jit(solution)/shard_map/reduce_scatter | solution.py:148
  266.0 7.8 copy-start.11
  270.6 3.2 copy-start.2
  282.1 39.4 %copy-start.5 = (s32[128,8]{0,1:T(8,128)S(1)}, s32[128,8]{0,1:T(8,128)}, u32[]{:S(2)}) copy-start(s32[128,8]{0,1:T(8,128)} %param.21) | copy-start | bytes 12292
  322.0 20.4 %copy-start.4 = (bf16[128,1024]{1,0:T(8,128)(2,1)S(1)}, bf16[128,1024]{1,0:T(8,128)(2,1)}, u32[]{:S(2)}) copy-start(bf16[128,1024]{1,0:T(8,128)(2,1)} %param.18) | copy-start | bytes 786436
  322.0 21.6 %copy-start.7 = (f32[1024]{0:T(1024)S(1)}, f32[1024]{0:T(1024)}, u32[]{:S(2)}) copy-start(f32[1024]{0:T(1024)} %param.23) | copy-start | bytes 12292
  366.9 191.9 %all-to-all-start = ((bf16[16,4,32,2048]{3,2,1,0:T(8,128)(2,1)}), bf16[16,4,32,2048]{3,2,1,0:T(8,128)(2,1)}, u32[]{:S(2)}, u32[]{:S(2)}) async-start(bf16[16,4,32,2048]{3,2,1,0:T(8,128)(2,1)} %bitcast.130), calls=%async_computation.1 | async-start | bytes 16777216 | tf_op jit(solution)/shard_map/all_to_all | solution.py:180
  376.4 319.4 %reduce-scatter.5.cloned.1.call-start = ((), (), s32[]{:S(2)}) async-start(), calls=%async_computation.11 | async-start | bytes 12582912 | tf_op jit(solution)/shard_map/reduce_scatter | solution.py:220
  590.3 4.3 copy-start.3
  695.8 98.8 %all-to-all-start.1 = ((bf16[16,4,32,1024]{3,2,1,0:T(8,128)(2,1)}), bf16[16,4,32,1024]{3,2,1,0:T(8,128)(2,1)}, u32[]{:S(2)}, u32[]{:S(2)}) async-start(bf16[16,4,32,1024]{3,2,1,0:T(8,128)(2,1)} %reduce-scatter.5.cloned.1.call-done), calls=%async_computation.3 | async-start | bytes 8388608 | tf_op jit(solution)/shard_map/all_to_all | solution.py:223
  794.6 9.8 %copy-start.1 = (f32[1024,64]{0,1:T(8,128)S(1)}, f32[1024,64]{0,1:T(8,128)}, u32[]{:S(2)}) copy-start(f32[1024,64]{0,1:T(8,128)} %param.30) | copy-start | bytes 786436
Sparse Core Ops, SparseCore 0:
  9.5 51.3 all-gather.8
  63.1 49.0 all-gather.6
  114.3 49.0 all-gather.12
  165.4 49.0 all-gather.10
  216.5 49.0 all-gather.14
  267.6 49.8 all-gather.16
  321.6 20.7 reduce-scatter.2
  597.0 98.7 reduce-scatter.4
where the time goes:
time: 813 us; the launch traced here: 811 us
  waiting for transfers between devices  612 us (75%)
  local copies, waits for them, and re-layouts  79.6 us (10%)
  matrix products  53.6 us (7%)
  blocking collectives  19.5 us (2%)
  between operations  16.5 us (2%)
  starting transfers between devices  16.2 us (2%)
  other arithmetic  14 us (2%)
    all_to_all x1, waiting for transfers between devices, local(): lax.all_to_all(sending, 'dp', split_axis=0, concat_axis=0, tiled=True)  153 us
    reduce_scatter x1, waiting for transfers between devices, local(): lax.psum_scatter(partial_rows.astype(jnp.bfloat16), 'mp', scatter_dimensi...  98.9 us
    all_to_all x1, waiting for transfers between devices, local(): lax.all_to_all(summed_rows, 'dp', split_axis=0, concat_axis=0, tiled=True)  84.9 us
    all_gather x1, waiting for transfers between devices, local(): value_piece = lax.all_gather(value_heads, 'dp', axis=0, tiled=True)  51.1 us
    all_gather x1, waiting for transfers between devices, local(): lax.all_gather(query_weight, 'dp', axis=0, tiled=True)  47.8 us
    all_gather x1, waiting for transfers between devices, local(): lax.all_gather(value_weight, 'dp', axis=0, tiled=True)  44.8 us
    all_gather x1, waiting for transfers between devices, local(): key_piece = lax.all_gather(key_heads, 'dp', axis=0, tiled=True)  43.5 us
    all_gather x1, waiting for transfers between devices, local(): lax.all_gather(key_weight, 'dp', axis=0, tiled=True)  41 us
  transfers between devices with their start and end apart: 10, of which 10 were waited for; matrix products, arithmetic and copies ran while one was open for 10% of the time, Pallas kernels for 0%

commit v1 on v0

--- a/solution.py
+++ b/solution.py
@@ -103,8 +103,11 @@
         jnp.zeros((local_heads, tok_rows), jnp.float32),
         jnp.zeros((tok_rows, local_heads, HEAD_DIM), jnp.float32),
     )
-    key_piece = lax.all_gather(key_heads, "dp", axis=0, tiled=True)
-    value_piece = lax.all_gather(value_heads, "dp", axis=0, tiled=True)
+    key_piece, value_piece = jnp.split(
+        lax.all_gather(jnp.concatenate([key_heads, value_heads], axis=1), "dp", axis=0, tiled=True),
+        [key_heads.shape[1]],
+        axis=1,
+    )
     piece_rows = key_piece.shape[0]
     key_seg, unused_pos, key_row = segment_info(lengths, jnp.int32(0), piece_rows)
 

time: 813 us -> 788 us (0.969)
  waiting for transfers between devices: 612 us -> 574 us
  local copies, waits for them, and re-layouts: 79.6 us -> 95.9 us
    all_gather x2 -> x1, waiting for transfers between devices: 94.6 us -> 69.1 us  [local(): lax.all_gather(jnp.concatenate([key_heads, value_heads], axis=1), 'dp', a...]
    all_gather x1, waiting for transfers between devices: 35.4 us -> 22.3 us  [local(): lax.all_gather(output_weight, 'dp', axis=1, tiled=True)]
    another operation x0 -> x1, local copies, waits for them, and re-layouts: none -> 12.4 us
  transfers between devices with their start and end apart: 10 -> 9, of which waited for: 10 -> 9; matrix products, arithmetic and copies ran while one was open for 10% -> 11% of each run, Pallas kernels for 0% -> 0%
where the time goes in v1:
time: 788 us; the launch traced here: 786 us
  waiting for transfers between devices  574 us (73%)
  local copies, waits for them, and re-layouts  95.9 us (12%)
  matrix products  50.1 us (6%)
  blocking collectives  19.5 us (2%)
  between operations  16.4 us (2%)
  starting transfers between devices  16.1 us (2%)
  other arithmetic  14.4 us (2%)
    all_to_all x1, waiting for transfers between devices, local(): lax.all_to_all(sending, 'dp', split_axis=0, concat_axis=0, tiled=True)  153 us
    reduce_scatter x1, waiting for transfers between devices, local(): lax.psum_scatter(partial_rows.astype(jnp.bfloat16), 'mp', scatter_dimensi...  98.8 us
    all_to_all x1, waiting for transfers between devices, local(): lax.all_to_all(summed_rows, 'dp', split_axis=0, concat_axis=0, tiled=True)  84.9 us
    all_gather x1, waiting for transfers between devices, local(): lax.all_gather(jnp.concatenate([key_heads, value_heads], axis=1), 'dp', a...  69.1 us
    all_gather x1, waiting for transfers between devices, local(): lax.all_gather(query_weight, 'dp', axis=0, tiled=True)  47.8 us
    all_gather x1, waiting for transfers between devices, local(): lax.all_gather(value_weight, 'dp', axis=0, tiled=True)  45.4 us
    all_gather x1, waiting for transfers between devices, local(): lax.all_gather(key_weight, 'dp', axis=0, tiled=True)  41 us
    all_gather x1, waiting for transfers between devices, local(): lax.all_gather(output_weight, 'dp', axis=1, tiled=True)  22.3 us
  transfers between devices with their start and end apart: 9, of which 9 were waited for; matrix products, arithmetic and copies ran while one was open for 11% of the time, Pallas kernels for 0%

profile of v1, /device:TPU:13, one launch (start us, length us, event | category | flops | bytes accessed | tf_op | source)
XLA Modules:
  0.0 786.3 jit_solution(17624591800150043721)
XLA Ops:
  6.5 0.7 all-gather.8.cloned.1.call-update
  7.3 0.7 all-gather.6.cloned.1.call-update
  8.1 0.7 all-gather.10.cloned.1.call-update
  8.8 0.8 reduce-window.8
  9.7 0.7 bitcast_subtract_fusion
  10.5 0.3 multiply_cosine_fusion
  10.9 8.1 %all_gather.21 = bf16[128,2048]{1,0:T(8,128)(2,1)S(1)} all-gather(bf16[128,1024]{1,0:T(8,128)(2,1)} %param.18), channel_id=1, replica_groups=mesh['dp'=16,'mp'=2] {'mp'}, dimensions={1}, use_global_device_ids=true | all-gather | bytes 786432 | tf_op jit(solution)/shard_map/all_gather | solution.py:70
  19.0 0.2 fusion.33
  19.2 0.7 broadcast_bitcast_fusion
  19.9 41.0 %all-gather.8.cloned.1.call-done = bf16[2048,1024]{1,0:T(8,128)(2,1)} async-done(((bf16[128,1024]{1,0:T(8,128)(2,1)}), bf16[2048,1024]{1,0:T(8,128)(2,1)}) %all-gather.8.cloned.1.call-update) | async-done | bytes 4194320 | tf_op jit(solution)/shard_map/all_gather | solution.py:85
  60.9 3.0 fusion.56
  64.0 0.2 multiply_reduce_fusion
  64.4 47.8 %all-gather.6.cloned.1.call-done = bf16[2048,1024]{1,0:T(8,128)(2,1)} async-done(((bf16[128,1024]{1,0:T(8,128)(2,1)}), bf16[2048,1024]{1,0:T(8,128)(2,1)}) %all-gather.6.cloned.1.call-update) | async-done | bytes 4194320 | tf_op jit(solution)/shard_map/all_gather | solution.py:80
  112.2 2.9 fusion.58
  115.2 0.2 multiply_reduce_fusion.1
  115.5 0.1 copy.97
  115.6 0.2 multiply_multiply_fusion
  115.8 0.2 multiply_multiply_fusion.1
  116.0 0.4 slice_negate_fusion
  116.4 0.4 maximum_multiply_fusion.1
  116.8 0.2 mul.217
  117.0 0.2 mul.239
  117.2 0.8 fusion.45
  118.0 45.4 %all-gather.10.cloned.1.call-done = bf16[2048,1024]{1,0:T(8,128)(2,1)} async-done(((bf16[128,1024]{1,0:T(8,128)(2,1)}), bf16[2048,1024]{1,0:T(8,128)(2,1)}) %all-gather.10.cloned.1.call-update) | async-done | bytes 4194320 | tf_op jit(solution)/shard_map/all_gather | solution.py:90
  163.4 2.9 convolution_convert_fusion
  166.4 0.9 pad_maximum_fusion
  167.3 0.5 all-gather.14.cloned.1.call-update
  168.0 0.6 fusion.61
  171.1 69.1 %all-gather.12.cloned.1.call-done = bf16[2048,2048]{1,0:T(8,128)(2,1)} async-done(((bf16[128,2048]{1,0:T(8,128)(2,1)}), bf16[2048,2048]{1,0:T(8,128)(2,1)}) %all-gather.12.cloned.1.call-update) | async-done | bytes 8388624 | tf_op jit(solution)/shard_map/all_gather | solution.py:107
  240.2 30.0 %conditional.1 = (f32[8,128]{1,0:T(8,128)S(1)}, f32[128,8,128]{0,2,1:T(8,128)S(1)}) conditional(s32[]{:T(128)} %bitcast.6, () %tuple.13, (s32[128]{0:T(128)S(1)}, s32[2048]{0:T(1024)S(1)}, s32[2048]{0:T(1024)S(1)}, s32[]{:T(128)}, s32[128]{0:T(128)S(1)}, /*index=5*/s32[2048]{0:T(1024)S(1)}, bf16[128,1024]{1,0:T(8,128)(2,1)S(1)}, ...), branch_computations={%region_7.8_spmd, %region_8.11_spmd} | conditional | flops 1102187648 | bytes 103610416 | solution.py:140
  240.2 0.4 or_and_fusion
  240.6 12.4 %copy.100 = bf16[2048,2048]{0,1:T(8,128)(2,1)} copy(bf16[2048,2048]{1,0:T(8,128)(2,1)} %get-tuple-element.80) | data formatting | bytes 16777216 | tf_op jit(solution)/shard_map
  253.0 3.9 fusion.60
  256.9 2.2 fusion
  259.1 3.2 copy-done.2
  262.3 2.9 fusion.9
  265.3 0.2 copy.124
  265.5 4.7 fusion.2
  270.2 22.3 %all-gather.14.cloned.1.call-done = bf16[1024,2048]{1,0:T(8,128)(2,1)} async-done(((bf16[1024,128]{1,0:T(8,128)(2,1)}), bf16[1024,2048]{1,0:T(8,128)(2,1)}) %all-gather.14.cloned.1.call-update) | async-done | bytes 4194320 | tf_op jit(solution)/shard_map/all_gather | solution.py:148
  292.5 3.9 fusion.63
  296.8 0.2 reduce_window_sum.19
  297.0 7.1 gather_fusion.2
  304.6 4.3 scatter_custom_fusion
  308.9 8.4 %reduce-scatter.3.cloned.1.call-done = f32[128,1024]{1,0:T(8,128)} async-done(((f32[128,2048]{1,0:T(8,128)}), f32[128,1024]{1,0:T(8,128)}) %reduce-scatter.3.cloned.1.call-update) | async-done | bytes 524304 | tf_op jit(solution)/shard_map/reduce_scatter | solution.py:151
  317.4 1.2 fusion.43
  318.6 0.7 fusion.36
  319.3 5.5 all-reduce.1
  324.9 5.9 all_gather.27
  330.9 11.0 %gather_fusion = bf16[2048,2048]{1,0:T(8,128)(2,1)} fusion(bf16[129,2048]{1,0:T(8,128)(2,1)S(1)} %concatenate.23, s32[2048]{0:T(1024)S(1)} %fusion.51), kind=kCustom, calls=%fused_computation | custom fusion | bytes 16785408 | tf_op jit(solution)/shard_map/gather | solution.py:182
  341.9 9.5 %all-to-all-start = ((bf16[16,4,32,2048]{3,2,1,0:T(8,128)(2,1)}), bf16[16,4,32,2048]{3,2,1,0:T(8,128)(2,1)}, u32[]{:S(2)}, u32[]{:S(2)}) async-start(bf16[16,4,32,2048]{3,2,1,0:T(8,128)(2,1)} %bitcast.114), calls=%async_computation.1 | async-start | bytes 16777216 | tf_op jit(solution)/shard_map/all_to_all | solution.py:183
  351.5 14.4 %reshape_squeeze.10 = bf16[2048,2,1024]{2,1,0:T(2,128)(2,1)} reshape(bf16[1,2048,2048]{2,1,0:T(8,128)(2,1)} %param.32) | data formatting | bytes 16777216 | tf_op jit(solution)/shard_map/reshape;squeeze | solution.py:209
  365.9 14.5 %reshape_squeeze.9 = bf16[2048,2,1024]{2,1,0:T(2,128)(2,1)} reshape(bf16[1,2048,2048]{2,1,0:T(8,128)(2,1)} %param.31) | data formatting | bytes 16777216 | tf_op jit(solution)/shard_map/reshape;squeeze | solution.py:203
  380.4 153.4 %all-to-all-done = bf16[16,4,32,2048]{3,2,1,0:T(8,128)(2,1)} async-done(((bf16[16,4,32,2048]{3,2,1,0:T(8,128)(2,1)}), bf16[16,4,32,2048]{3,2,1,0:T(8,128)(2,1)}, u32[]{:S(2)}, u32[]{:S(2)}) %all-to-all-start) | async-done | bytes 8388640 | tf_op jit(solution)/shard_map/all_to_all | solution.py:183
  533.8 11.3 %fusion.18 = f32[2,16,32,1024]{3,2,1,0:T(8,128)} fusion(bf16[2048,2,1024,1]{2,1,0,3:T(2,128)(2,1)} %bitcast.117, bf16[16,4,32,2048]{3,2,1,0:T(8,128)(2,1)} %all-to-all-done, s32[]{:T(128)S(6)} %select_n.52), kind=kOutput, calls=%fused_computation.25 | convolution fusion | flops 4294967296 | bytes 16777220 | tf_op jit(solution)/shard_map/secd,def->secf/dot_general | solution.py:206
  545.1 20.3 %convolution_bitcast_fusion = bf16[16,2,32,2048]{3,2,0,1:T(8,128)(2,1)} fusion(bf16[2,1024,2048,1]{2,1,3,0:T(8,128)(2,1)} %bitcast.133, f32[2,16,32,1024]{3,2,1,0:T(8,128)} %fusion.18, bf16[2048,2,1024,1]{2,1,0,3:T(2,128)(2,1)} %bitcast.116, bf16[16,4,32,2048]{3,2,1,0:T(8,128)(2,1)} %all-to-all-done, s32[]{:T(128)S(6)} %select_n.52), kind=kOutput, calls=%fused_computation.30 | convolution fusion | flops 8596226048 | bytes 29360132 | tf_op jit(solution)/shard_map/secf,efd->secd/dot_general | solution.py:213
  565.3 4.3 broadcast_in_dim.70
  569.6 2.3 copy_dynamic-update-slice_fusion
  571.9 98.8 %reduce-scatter.5.cloned.1.call-done = bf16[16,4,32,1024]{3,2,1,0:T(8,128)(2,1)} async-done(((bf16[16,4,32,2048]{3,2,1,0:T(8,128)(2,1)}), bf16[16,4,32,1024]{3,2,1,0:T(8,128)(2,1)}) %reduce-scatter.5.cloned.1.call-update) | async-done | bytes 4194320 | tf_op jit(solution)/shard_map/reduce_scatter | solution.py:223
  670.8 6.4 all-to-all-start.1
  677.4 7.0 gather_fusion.3
  684.7 84.9 %all-to-all-done.1 = bf16[16,4,32,1024]{3,2,1,0:T(8,128)(2,1)} async-done(((bf16[16,4,32,1024]{3,2,1,0:T(8,128)(2,1)}), bf16[16,4,32,1024]{3,2,1,0:T(8,128)(2,1)}, u32[]{:S(2)}, u32[]{:S(2)}) %all-to-all-start.1) | async-done | bytes 4194336 | tf_op jit(solution)/shard_map/all_to_all | solution.py:226
  769.6 7.7 gather_fusion.1
  777.4 1.3 fusion.22
  778.7 0.8 fusion.44
  (80 shorter events, 2.7 us)
Async XLA Ops:
  6.5 312.1 %copy-start = (f32[1024,64]{0,1:T(8,128)S(1)}, f32[1024,64]{0,1:T(8,128)}, u32[]{:S(2)}) copy-start(f32[1024,64]{0,1:T(8,128)} %param.30) | copy-start | bytes 786436
  6.5 54.4 %all-gather.8.cloned.1.call-start = ((), (), s32[]{:S(2)}) async-start(), calls=%async_computation.5 | async-start | bytes 4456448 | tf_op jit(solution)/shard_map/all_gather | solution.py:85
  7.3 104.9 %all-gather.6.cloned.1.call-start = ((), (), s32[]{:S(2)}) async-start(), calls=%async_computation.4 | async-start | bytes 4456448 | tf_op jit(solution)/shard_map/all_gather | solution.py:80
  8.0 155.4 %all-gather.10.cloned.1.call-start = ((), (), s32[]{:S(2)}) async-start(), calls=%async_computation.6 | async-start | bytes 4456448 | tf_op jit(solution)/shard_map/all_gather | solution.py:90
  8.7 231.5 %all-gather.12.cloned.1.call-start = ((), (), s32[]{:S(2)}) async-start(), calls=%async_computation.7 | async-start | bytes 8912896 | tf_op jit(solution)/shard_map/all_gather | solution.py:107
  10.9 101.2 %copy-start.6 = (f32[2048]{0:T(1024)S(1)}, f32[2048]{0:T(1024)}, u32[]{:S(2)}) copy-start(f32[2048]{0:T(1024)} %param.22) | copy-start | bytes 24580
  63.9 51.7 %copy-start.9 = (f32[128]{0:T(128)S(1)}, f32[128]{0:T(128)}, u32[]{:S(2)}) copy-start(f32[128]{0:T(128)} %param.25) | copy-start | bytes 1540
  64.2 51.6 %copy-start.10 = (f32[128]{0:T(128)S(1)}, f32[128]{0:T(128)}, u32[]{:S(2)}) copy-start(f32[128]{0:T(128)} %param.24) | copy-start | bytes 1540
  118.0 122.2 %copy-start.8 = (s32[2048]{0:T(1024)S(1)}, s32[2048]{0:T(1024)}, u32[]{:S(2)}) copy-start(s32[2048]{0:T(1024)} %param.20) | copy-start | bytes 24580
  167.3 125.2 %all-gather.14.cloned.1.call-start = ((), (), s32[]{:S(2)}) async-start(), calls=%async_computation.8 | async-start | bytes 4456448 | tf_op jit(solution)/shard_map/all_gather | solution.py:148
  167.9 149.5 %reduce-scatter.3.cloned.1.call-start = ((), (), s32[]{:S(2)}) async-start(), calls=%async_computation.9 | async-start | bytes 1572864 | tf_op jit(solution)/shard_map/reduce_scatter | solution.py:151
  259.1 3.2 copy-start.2
  270.2 26.3 %copy-start.5 = (s32[128,8]{0,1:T(8,128)S(1)}, s32[128,8]{0,1:T(8,128)}, u32[]{:S(2)}) copy-start(s32[128,8]{0,1:T(8,128)} %param.21) | copy-start | bytes 12292
  297.0 20.4 %copy-start.4 = (bf16[128,1024]{1,0:T(8,128)(2,1)S(1)}, bf16[128,1024]{1,0:T(8,128)(2,1)}, u32[]{:S(2)}) copy-start(bf16[128,1024]{1,0:T(8,128)(2,1)} %param.18) | copy-start | bytes 786436
  297.0 21.6 %copy-start.7 = (f32[1024]{0:T(1024)S(1)}, f32[1024]{0:T(1024)}, u32[]{:S(2)}) copy-start(f32[1024]{0:T(1024)} %param.23) | copy-start | bytes 12292
  341.9 191.9 %all-to-all-start = ((bf16[16,4,32,2048]{3,2,1,0:T(8,128)(2,1)}), bf16[16,4,32,2048]{3,2,1,0:T(8,128)(2,1)}, u32[]{:S(2)}, u32[]{:S(2)}) async-start(bf16[16,4,32,2048]{3,2,1,0:T(8,128)(2,1)} %bitcast.114), calls=%async_computation.1 | async-start | bytes 16777216 | tf_op jit(solution)/shard_map/all_to_all | solution.py:183
  351.4 319.3 %reduce-scatter.5.cloned.1.call-start = ((), (), s32[]{:S(2)}) async-start(), calls=%async_computation.10 | async-start | bytes 12582912 | tf_op jit(solution)/shard_map/reduce_scatter | solution.py:223
  565.3 4.3 copy-start.3
  670.8 98.8 %all-to-all-start.1 = ((bf16[16,4,32,1024]{3,2,1,0:T(8,128)(2,1)}), bf16[16,4,32,1024]{3,2,1,0:T(8,128)(2,1)}, u32[]{:S(2)}, u32[]{:S(2)}) async-start(bf16[16,4,32,1024]{3,2,1,0:T(8,128)(2,1)} %reduce-scatter.5.cloned.1.call-done), calls=%async_computation.3 | async-start | bytes 8388608 | tf_op jit(solution)/shard_map/all_to_all | solution.py:226
  769.6 9.8 %copy-start.1 = (f32[1024,64]{0,1:T(8,128)S(1)}, f32[1024,64]{0,1:T(8,128)}, u32[]{:S(2)}) copy-start(f32[1024,64]{0,1:T(8,128)} %param.30) | copy-start | bytes 786436
Sparse Core Ops, SparseCore 0:
  9.5 51.3 all-gather.7
  63.1 49.0 all-gather.5
  114.3 49.0 all-gather.9
  167.4 72.7 all-gather.11
  242.2 50.2 all-gather.13
  296.6 20.7 reduce-scatter.2
  572.1 98.6 reduce-scatter.4
